TPU v7x, 32 devices: a whole 2x2x4 slice. The times are simulated.
32 devices in a mesh: groups: 2 (over y), ctx: 16 (over z, x, core).
Axes of the slice: x: 2, y: 2, z: 4, core: 2. Of those that a mesh axis runs over, the one named last changes fastest.
Arguments:
- queries: bfloat16 [16384, 2048], P(('groups', 'ctx')), parts along dimension 0, may hold values from -60 to 60
- keys: bfloat16 [16384, 512], P(('groups', 'ctx')), parts along dimension 0, may hold values from -30 to 30
- values: bfloat16 [16384, 512], P(('groups', 'ctx')), parts along dimension 0, may hold values from -24 to 24
- block_lengths: int32 [32], P(('groups', 'ctx')), parts along dimension 0, may hold values from 256 to 512, as said below
- out_weight: bfloat16 [2048, 4096], P(None, 'ctx'), may hold values from -0.125 to 0.125
Outputs:
- hidden_states: bfloat16 [16384, 4096], P(('groups', 'ctx')), parts along dimension 0
There are 2 independent parts, one for each index of `groups`. A program takes and returns all parts, laid end to end along the dimension named above; an argument that names none is the same for every part. Nothing has to cross between parts.
Inputs may be any that keep to these rules, and one draw needn't show every extreme that they name: `block_lengths`: block 0 always holds 512 valid tokens.
All inputs are finite; a program needn't handle non-finite values.
Results may differ from a plain program's by a relative error of at most 0.0057.
Values may be sent and summed in bfloat16 or wider, within the bound.
A program may use at most 128 MiB of HBM per device.

v0:
```python
import math

import jax
import jax.numpy as jnp
from jax import lax
from jax.sharding import PartitionSpec as P

HD = 128


def broadcast(block, axis, source):
    block = jnp.where(lax.axis_index(axis) == source, block, jnp.zeros_like(block))
    return lax.psum(block, axis)


def make_mask(row_count, valid_length, has_anchor):
    row_ids = jnp.arange(row_count)[:, None]
    col_ids = jnp.arange(row_count)[None, :]
    local_mask = (col_ids <= row_ids) & (col_ids < valid_length)
    anchor_mask = jnp.broadcast_to(has_anchor, (row_count, row_count))
    return jnp.concatenate([anchor_mask, local_mask], axis=1)


def attend(query_rows, key_rows, value_rows, anchor_keys, anchor_values, valid_length, has_anchor):
    row_count = query_rows.shape[0]
    key_heads = key_rows.shape[1] // HD
    group_size = query_rows.shape[1] // key_rows.shape[1]
    query_stack = query_rows.reshape(row_count, key_heads, group_size, HD).transpose(1, 0, 2, 3)
    key_stack = (
        jnp.concatenate([anchor_keys, key_rows], axis=0)
        .reshape(2 * row_count, key_heads, HD)
        .transpose(1, 0, 2)
    )
    value_stack = (
        jnp.concatenate([anchor_values, value_rows], axis=0)
        .reshape(2 * row_count, key_heads, HD)
        .transpose(1, 0, 2)
    )
    visible = make_mask(row_count, valid_length, has_anchor)

    def one_head(operands):
        head_queries, head_keys, head_values = operands
        scores = jnp.einsum(
            "qgd,kd->gqk", head_queries, head_keys, preferred_element_type=jnp.float32
        ) / math.sqrt(HD)
        scores = jnp.where(visible[None], scores, -jnp.inf)
        row_top = jnp.max(scores, axis=-1, keepdims=True)
        exponent = jnp.exp(scores - row_top)
        soft_weights = (exponent / jnp.sum(exponent, axis=-1, keepdims=True)).astype(jnp.bfloat16)
        mixture = jnp.einsum(
            "gqk,kd->qgd", soft_weights, head_values, preferred_element_type=jnp.float32
        )
        return mixture.astype(jnp.bfloat16)

    stacked = lax.map(one_head, (query_stack, key_stack, value_stack))
    return stacked.transpose(1, 0, 2, 3).reshape(row_count, key_heads * group_size * HD)


def per_device(queries, keys, values, block_lengths, out_weight):
    has_anchor = lax.axis_index("ctx") > 0
    anchor_keys, anchor_values = (broadcast(keys, "ctx", 0), broadcast(values, "ctx", 0))
    mixture = attend(
        queries, keys, values, anchor_keys, anchor_values, block_lengths[0], has_anchor
    )
    output = jnp.dot(
        mixture,
        lax.all_gather(out_weight, "ctx", axis=1, tiled=True),
        preferred_element_type=jnp.float32,
    )
    return output.astype(jnp.bfloat16)


def solution(mesh):
    return jax.shard_map(
        per_device,
        mesh=mesh,
        in_specs=(
            P(("groups", "ctx"), None),
            P(("groups", "ctx"), None),
            P(("groups", "ctx"), None),
            P(("groups", "ctx")),
            P(None, "ctx"),
        ),
        out_specs=P(("groups", "ctx"), None),
        check_vma=False,
    )
```

profile of v0, /device:TPU:25, one launch (start us, length us, event | category | flops | bytes accessed | tf_op | source)
XLA Modules:
  0.0 256.8 jit_solution(13996809299489624549)
XLA Ops:
  6.5 1.4 copy.11
  7.9 1.3 copy.9
  9.2 1.1 broadcast_select_fusion
  10.3 0.0 all-reduce.4.cloned.1.call-update
  10.3 0.0 all-gather.2.cloned.1.call-start
  10.4 0.7 all-gather.2.cloned.1.call-update
  11.7 0.0 copy-done
  11.7 2.5 copy.13
  14.3 0.1 fusion.39
  14.4 0.9 concatenate.10
  15.3 87.3 %all-reduce.4.cloned.1.call-done = (bf16[512,512]{0,1:T(8,128)(2,1)}, bf16[512,512]{0,1:T(8,128)(2,1)}) async-done(((bf16[512,512]{0,1:T(8,128)(2,1)}, bf16[512,512]{0,1:T(8,128)(2,1)}), (bf16[512,512]{0,1:T(8,128)(2,1)}, bf16[512,512]{0,1:T(8,128)(2,1)})) %all-reduce.4.cloned.1.call-update) | async-done | bytes 1048592 | tf_op jit(solution)/shard_map/psum | solution.py:13
  102.6 1.2 pad_maximum_fusion.1
  103.8 1.2 pad_maximum_fusion
  105.0 50.3 %while.10 = (s32[]{:T(128)}, bf16[4,512,4,128]{1,3,2,0:T(8,128)(2,1)}, bf16[4,1024,128]{1,2,0:T(8,128)(2,1)S(1)}, pred[512,1024]{0,1:T(8,128)(4,1)}, bf16[4,1024...) while((s32[]{:T(128)}, bf16[4,512,4,128]{1,3,2,0:T(8,128)(2,1)}, ...), condition=%wide.region_5.6_spmd, body=%wide.region_2.5_spmd.sunk | while | flops 1086587904 | bytes 18892876 | solution.py:55
  105.0 7.5 %fusion.59 = (f32[4,512]{1,0:T(4,128)S(1)}, f32[4,512,1024]{1,2,0:T(8,128)}) fusion(pred[512,1024]{0,1:T(8,128)(4,1)} %get-tuple-element.120, bf16[4,512,4,128]{1,3,2,0:T(8,128)(2,1)} %get-tuple-element.122, s32[]{:T(128)} %get-tuple-element.110, bf16[4,1024,128]{1,2,0:T(8,128)(2,1)S(1)} %get-tuple-element.121), kind=kOutput, calls=%fused_computation.37.clone.1 | convolution fusion | flops 545260544 | bytes 9708544 | tf_op jit(solution)/shard_map/while/body/eval_jaxpr/sub | solution.py:48
  112.5 5.6 %fusion.60 = bf16[4,512,4,128]{1,3,2,0:T(8,128)(2,1)} fusion(bf16[4,512,4,128]{1,3,2,0:T(8,128)(2,1)} %get-tuple-element.111, s32[]{:T(128)} %get-tuple-element.110, f32[4,512,1024]{1,2,0:T(8,128)} %get-tuple-element.101, f32[4,512]{1,0:T(4,128)S(1)} %get-tuple-element.102, bf16[4,1024,128]{1,2,0:T(8,128)(2,1)S(1)} %get-tuple-element.119), kind=kOutput, calls=%fused_computation.11.clone.1 | convolution fusion | flops 541327360 | bytes 9184256 | tf_op jit(solution)/shard_map/while/body/eval_jaxpr/gqk,kd->qgd/dot_general | solution.py:50
  118.0 7.5 %fusion.59 = (f32[4,512]{1,0:T(4,128)S(1)}, f32[4,512,1024]{1,2,0:T(8,128)}) fusion(pred[512,1024]{0,1:T(8,128)(4,1)} %get-tuple-element.120, bf16[4,512,4,128]{1,3,2,0:T(8,128)(2,1)} %get-tuple-element.122, s32[]{:T(128)} %get-tuple-element.110, bf16[4,1024,128]{1,2,0:T(8,128)(2,1)S(1)} %get-tuple-element.121), kind=kOutput, calls=%fused_computation.37.clone.1 | convolution fusion | flops 545260544 | bytes 9708544 | tf_op jit(solution)/shard_map/while/body/eval_jaxpr/sub | solution.py:48
  125.5 5.0 %fusion.60 = bf16[4,512,4,128]{1,3,2,0:T(8,128)(2,1)} fusion(bf16[4,512,4,128]{1,3,2,0:T(8,128)(2,1)} %get-tuple-element.111, s32[]{:T(128)} %get-tuple-element.110, f32[4,512,1024]{1,2,0:T(8,128)} %get-tuple-element.101, f32[4,512]{1,0:T(4,128)S(1)} %get-tuple-element.102, bf16[4,1024,128]{1,2,0:T(8,128)(2,1)S(1)} %get-tuple-element.119), kind=kOutput, calls=%fused_computation.11.clone.1 | convolution fusion | flops 541327360 | bytes 9184256 | tf_op jit(solution)/shard_map/while/body/eval_jaxpr/gqk,kd->qgd/dot_general | solution.py:50
  130.5 7.5 %fusion.59 = (f32[4,512]{1,0:T(4,128)S(1)}, f32[4,512,1024]{1,2,0:T(8,128)}) fusion(pred[512,1024]{0,1:T(8,128)(4,1)} %get-tuple-element.120, bf16[4,512,4,128]{1,3,2,0:T(8,128)(2,1)} %get-tuple-element.122, s32[]{:T(128)} %get-tuple-element.110, bf16[4,1024,128]{1,2,0:T(8,128)(2,1)S(1)} %get-tuple-element.121), kind=kOutput, calls=%fused_computation.37.clone.1 | convolution fusion | flops 545260544 | bytes 9708544 | tf_op jit(solution)/shard_map/while/body/eval_jaxpr/sub | solution.py:48
  138.0 4.9 %fusion.60 = bf16[4,512,4,128]{1,3,2,0:T(8,128)(2,1)} fusion(bf16[4,512,4,128]{1,3,2,0:T(8,128)(2,1)} %get-tuple-element.111, s32[]{:T(128)} %get-tuple-element.110, f32[4,512,1024]{1,2,0:T(8,128)} %get-tuple-element.101, f32[4,512]{1,0:T(4,128)S(1)} %get-tuple-element.102, bf16[4,1024,128]{1,2,0:T(8,128)(2,1)S(1)} %get-tuple-element.119), kind=kOutput, calls=%fused_computation.11.clone.1 | convolution fusion | flops 541327360 | bytes 9184256 | tf_op jit(solution)/shard_map/while/body/eval_jaxpr/gqk,kd->qgd/dot_general | solution.py:50
  142.9 7.5 %fusion.59 = (f32[4,512]{1,0:T(4,128)S(1)}, f32[4,512,1024]{1,2,0:T(8,128)}) fusion(pred[512,1024]{0,1:T(8,128)(4,1)} %get-tuple-element.120, bf16[4,512,4,128]{1,3,2,0:T(8,128)(2,1)} %get-tuple-element.122, s32[]{:T(128)} %get-tuple-element.110, bf16[4,1024,128]{1,2,0:T(8,128)(2,1)S(1)} %get-tuple-element.121), kind=kOutput, calls=%fused_computation.37.clone.1 | convolution fusion | flops 545260544 | bytes 9708544 | tf_op jit(solution)/shard_map/while/body/eval_jaxpr/sub | solution.py:48
  150.4 4.9 %fusion.60 = bf16[4,512,4,128]{1,3,2,0:T(8,128)(2,1)} fusion(bf16[4,512,4,128]{1,3,2,0:T(8,128)(2,1)} %get-tuple-element.111, s32[]{:T(128)} %get-tuple-element.110, f32[4,512,1024]{1,2,0:T(8,128)} %get-tuple-element.101, f32[4,512]{1,0:T(4,128)S(1)} %get-tuple-element.102, bf16[4,1024,128]{1,2,0:T(8,128)(2,1)S(1)} %get-tuple-element.119), kind=kOutput, calls=%fused_computation.11.clone.1 | convolution fusion | flops 541327360 | bytes 9184256 | tf_op jit(solution)/shard_map/while/body/eval_jaxpr/gqk,kd->qgd/dot_general | solution.py:50
  155.3 80.2 %all-gather.2.cloned.1.call-done = bf16[2048,4096]{1,0:T(8,128)(2,1)} async-done(((bf16[2048,256]{1,0:T(8,128)(2,1)}), bf16[2048,4096]{1,0:T(8,128)(2,1)}) %all-gather.2.cloned.1.call-update) | async-done | bytes 16777232 | tf_op jit(solution)/shard_map/all_gather | solution.py:67
  235.5 14.5 %convolution_convert_fusion = bf16[512,4096]{1,0:T(8,128)(2,1)} fusion(bf16[512,2048]{0,1:T(8,128)(2,1)} %bitcast.77, bf16[2048,4096]{1,0:T(8,128)(2,1)} %all-gather.2.cloned.1.call-done), kind=kOutput, calls=%fused_computation.29 | convolution fusion | flops 8592031744 | bytes 23068672 | tf_op jit(solution)/shard_map/dot_general | solution.py:65
  (4 shorter events, 0.0 us)
Async XLA Ops:
  6.5 5.2 %copy-start = (bf16[512,2048]{1,0:T(8,128)(2,1)S(1)}, bf16[512,2048]{1,0:T(8,128)(2,1)}, u32[]{:S(2)}) copy-start(bf16[512,2048]{1,0:T(8,128)(2,1)} %param.7) | copy-start | bytes 6291460
  6.5 96.1 %all-reduce.4.cloned.1.call-start = ((), (), s32[]{:S(2)}) async-start(), calls=%async_computation.1 | async-start | bytes 2097152 | tf_op jit(solution)/shard_map/psum | solution.py:13
  10.3 225.2 %all-gather.2.cloned.1.call-start = ((), (), s32[]{:S(2)}) async-start(), calls=%async_computation | async-start | bytes 17825792 | tf_op jit(solution)/shard_map/all_gather | solution.py:67
Sparse Core Ops, SparseCore 0:
  10.9 91.6 all-reduce.3
  104.7 130.6 all-gather.1
where the time goes:
time: 260 us; the launch traced here: 257 us
  waiting for transfers between devices  168 us (65%)
  matrix products  64.7 us (25%)
  between operations  14.1 us (5%)
  local copies, waits for them, and re-layouts  6.06 us (2%)
  other arithmetic  3.6 us (1%)
    psum x1, waiting for transfers between devices, broadcast(): return lax.psum(block, axis)  87.3 us
    all_gather x1, waiting for transfers between devices, per_device(): lax.all_gather(out_weight, 'ctx', axis=1, tiled=True)  80.2 us
    sub x4, matrix products, one_head(): exponent = jnp.exp(scores - row_top)  29.9 us
    dot_general x4, matrix products, one_head(): jnp.einsum('gqk,kd->qgd', soft_weights, head_values, preferred_element_ty...  20.4 us
    dot_general x1, matrix products, per_device(): jnp.dot(mixture, lax.all_gather(out_weight, 'ctx', axis=1, tiled=True), p...  14.5 us
  transfers between devices with their start and end apart: 2, of which 2 were waited for; matrix products, arithmetic and copies ran while one was open for 22% of the time, Pallas kernels for 0%

commit v1 on v0

--- a/solution.py
+++ b/solution.py
@@ -1,11 +1,331 @@
+import functools
 import math
 
 import jax
 import jax.numpy as jnp
 from jax import lax
+from jax.experimental import pallas as pl
+from jax.experimental.pallas import tpu as pltpu
 from jax.sharding import PartitionSpec as P
 
 HD = 128
+MESH = pl.DeviceIdType.MESH
+LOW = -1e30
+
+
+def kernel(n, ctx_axis, length_ref, q_hbm, k_hbm, v_hbm, w_hbm, out_ref, q_ref, k_ref, v_ref, ak_ref, av_ref, wbuf,
+           acc_ref, top_ref, sum_ref, mix_ref, ring_send, ring_recv, y_send, y_recv, sib_send, sib_recv,
+           anchor_send, anchor_recv, local_sem):
+    group = lax.axis_index("groups")
+    me = lax.axis_index("ctx")
+    chips = n // 2
+    half = chips // 2
+    core = me % 2
+    chip = me // 2
+    x = chip % 2
+    z = chip // 2
+    pos = (1 - x) * z + x * (chips - 1 - z)
+    rows, width = w_hbm.shape
+    tokens = q_ref.shape[0]
+    kv_heads = k_ref.shape[1] // HD
+    per_kv = q_ref.shape[1] // k_ref.shape[1]
+    scale = math.log2(math.e) / math.sqrt(HD)
+
+    def chip_at(p):
+        p = (p + chips) % chips
+        h = p // half
+        return (1 - h) * 2 * p + h * (2 * (chips - 1 - p) + 1)
+
+    right = (group, chip_at(pos + 1) * 2 + core)
+    left = (group, chip_at(pos - 1) * 2 + core)
+    other = (1 - group, me)
+    sibling = (group, me + 1 - 2 * core)
+    cross = (group, me + 2 - 4 * x)
+    above = (group, (me + 4) % n)
+
+    share = rows * 11 // 32 // 16 * 16
+    mine = pl.ds(pl.multiple_of(group * share, 16), share)
+    theirs = pl.ds(pl.multiple_of((1 - group) * share, 16), share)
+    common = pl.ds(2 * share, rows - 2 * share)
+    RIGHT, LEFT = 0, 1
+
+    def origin(d, s, c):
+        return chip_at(pos - s if d == RIGHT else pos + s) * 2 + c
+
+    def remote(src, dst, send, recv, device):
+        return pltpu.make_async_remote_copy(src_ref=src, dst_ref=dst, send_sem=send, recv_sem=recv,
+                                            device_id=device, device_id_type=MESH)
+
+    sent = []
+
+    def ring_copy(d, s, piece):
+        which = mine if piece == 0 else common
+        o = origin(d, s - 1, core)
+        src = (w_hbm if s == 1 else wbuf.at[o]).at[which]
+        return remote(src, wbuf.at[o].at[which], ring_send.at[d, s - 1, piece], ring_recv.at[d, s - 1, piece],
+                      right if d == RIGHT else left)
+
+    def has(d, s, piece):
+        if s < half:
+            return True
+        return s == half and piece == d
+
+    def start(copy):
+        copy.start()
+        sent.append(copy)
+
+    def sib_copy(d, s, part):
+        which = (mine, common, theirs)[part]
+        o = origin(d, s, core)
+        return remote(wbuf.at[o].at[which], wbuf.at[o].at[which], sib_send.at[d, s, part], sib_recv.at[d, s, part], sibling)
+
+    def y_copy(d, s):
+        o = origin(d, s, core)
+        return remote(wbuf.at[o].at[mine], wbuf.at[o].at[mine], y_send.at[d, s - 1], y_recv.at[d, s - 1], other)
+
+    own_sib = remote(w_hbm, wbuf.at[me], sib_send.at[0, 0, 0], sib_recv.at[0, 0, 0], sibling)
+
+    def serve_ring(s, piece):
+        for d in (RIGHT, LEFT):
+            if not has(d, s, piece):
+                continue
+            ring_copy(d, s, piece).wait_recv()
+            if has(d, s + 1, piece):
+                start(ring_copy(d, s + 1, piece))
+            if piece == 0:
+                start(y_copy(d, s))
+            start(sib_copy(d, s, piece))
+
+    def serve_y(s):
+        for d in (RIGHT, LEFT):
+            if has(d, s, 0):
+                y_copy(d, s).wait_recv()
+                start(sib_copy(d, s, 2))
+
+    root = me == 0
+
+    def anchor_copies(h):
+        k = h * 2 // kv_heads
+        cols = pl.ds(h * HD, HD)
+        lead = (core == 0) & (x == k)
+        z_cond = lead & (z < half - 1)
+        x_cond = lead if k == 0 else (lead & (z > 0)) | root
+        found = []
+        for kind, (cond, device) in enumerate(((z_cond, above), (x_cond, cross), (core == 0, sibling))):
+            for t, ref in enumerate((ak_ref, av_ref)):
+                view = ref.at[:, cols]
+                found.append((cond, remote(view, view, anchor_send.at[h, kind, t], anchor_recv.at[h, t], device)))
+        return found
+
+    def serve_anchor(h):
+        @pl.when(me > 0)
+        def _():
+            for t, ref in enumerate((ak_ref, av_ref)):
+                view = ref.at[:, pl.ds(h * HD, HD)]
+                remote(view, view, anchor_send.at[h, 0, t], anchor_recv.at[h, t], sibling).wait_recv()
+        send_anchor(h)
+
+    def send_anchor(h):
+        for cond, copy in anchor_copies(h):
+            @pl.when(cond)
+            def _():
+                copy.start()
+
+    loads = [
+        pltpu.make_async_copy(k_hbm, k_ref, local_sem.at[0]),
+        pltpu.make_async_copy(v_hbm, v_ref, local_sem.at[1]),
+        pltpu.make_async_copy(q_hbm, q_ref, local_sem.at[2]),
+        pltpu.make_async_copy(w_hbm, wbuf.at[me], local_sem.at[3]),
+    ]
+    for load in loads:
+        load.start()
+    root_loads = [
+        pltpu.make_async_copy(k_hbm, ak_ref, local_sem.at[4]),
+        pltpu.make_async_copy(v_hbm, av_ref, local_sem.at[5]),
+    ]
+
+    @pl.when(root)
+    def _():
+        for load in root_loads:
+            load.start()
+
+    barrier = pltpu.get_barrier_semaphore()
+    for device in (right, left, other, sibling, cross):
+        pl.semaphore_signal(barrier, inc=1, device_id=device, device_id_type=MESH)
+    pl.semaphore_wait(barrier, 5)
+
+    @pl.when(root)
+    def _():
+        for load in root_loads:
+            load.wait()
+        for h in range(kv_heads):
+            send_anchor(h)
+
+    for piece in (0, 1):
+        for d in (RIGHT, LEFT):
+            if has(d, 1, piece):
+                start(ring_copy(d, 1, piece))
+    start(own_sib)
+    for load in loads:
+        load.wait()
+
+    def serve_anchor_beyond_root(h):
+        @pl.when(me > 0)
+        def _():
+            for t, ref in enumerate((ak_ref, av_ref)):
+                view = ref.at[:, pl.ds(h * HD, HD)]
+                remote(view, view, anchor_send.at[h, 0, t], anchor_recv.at[h, t], sibling).wait_recv()
+            send_anchor(h)
+
+    last = length_ref[0] - 1
+    block = tokens // 2
+
+    def own_heads(j):
+        cols = pl.ds(j * HD, HD)
+
+        @pl.loop(0, per_kv)
+        def _(i):
+            h = j * per_kv + i
+            head = pl.ds(pl.multiple_of(h * HD, HD), HD)
+            for b in range(2):
+                seen = block * (b + 1)
+                rows_b = pl.ds(b * block, block)
+                s = lax.dot_general(q_ref[rows_b, head], k_ref[pl.ds(0, seen), cols], (((1,), (1,)), ((), ())),
+                                    preferred_element_type=jnp.float32)
+                row = lax.broadcasted_iota(jnp.int32, (block, 1), 0) + b * block
+                col = lax.broadcasted_iota(jnp.int32, (block, seen), 1)
+                s = jnp.where(col <= jnp.minimum(row, last), s, LOW)
+                top = jnp.max(s, axis=1, keepdims=True)
+                e = jnp.exp2((s - top) * scale)
+                top_ref[h, rows_b, :] = top
+                sum_ref[h, rows_b, :] = jnp.sum(e, axis=1, keepdims=True)
+                acc_ref[rows_b, head] = jnp.dot(e.astype(jnp.bfloat16), v_ref[pl.ds(0, seen), cols],
+                                                preferred_element_type=jnp.float32)
+
+    def anchor_heads(j):
+        cols = pl.ds(j * HD, HD)
+
+        @pl.when(me > 0)
+        def _():
+            @pl.loop(0, per_kv)
+            def _(i):
+                h = j * per_kv + i
+                head = pl.ds(pl.multiple_of(h * HD, HD), HD)
+                for b in range(2):
+                    rows_b = pl.ds(b * block, block)
+                    s = lax.dot_general(q_ref[rows_b, head], ak_ref[:, cols], (((1,), (1,)), ((), ())),
+                                        preferred_element_type=jnp.float32)
+                    old = top_ref[h, rows_b, :]
+                    top = jnp.maximum(old, jnp.max(s, axis=1, keepdims=True))
+                    e = jnp.exp2((s - top) * scale)
+                    keep = jnp.exp2((old - top) * scale)
+                    total = sum_ref[h, rows_b, :] * keep + jnp.sum(e, axis=1, keepdims=True)
+                    mixed = acc_ref[rows_b, head] * keep + jnp.dot(e.astype(jnp.bfloat16), av_ref[:, cols],
+                                                                   preferred_element_type=jnp.float32)
+                    mix_ref[rows_b, head] = (mixed * (1.0 / total)).astype(jnp.bfloat16)
+
+        @pl.when(me == 0)
+        def _():
+            @pl.loop(0, per_kv)
+            def _(i):
+                h = j * per_kv + i
+                head = pl.ds(pl.multiple_of(h * HD, HD), HD)
+                mix_ref[:, head] = (acc_ref[:, head] * (1.0 / sum_ref[h])).astype(jnp.bfloat16)
+
+    def project(o):
+        out_ref[:, pl.ds(pl.multiple_of(o * width, width), width)] = jnp.dot(
+            mix_ref[...], wbuf[o], preferred_element_type=jnp.float32).astype(out_ref.dtype)
+
+    def project_step(s):
+        count = 2 if s == half else 4
+        for d in (RIGHT, LEFT):
+            for piece in range(3):
+                if has(d, s, 1 if piece == 1 else 0):
+                    sib_copy(d, s, piece).wait_recv()
+
+        @pl.loop(0, count)
+        def _(i):
+            turn = 1 - 2 * (i // 2)
+            project(chip_at(pos - turn * s) * 2 + (i + core) % 2)
+
+    own_heads(0)
+    for h in range(kv_heads // 2):
+        serve_anchor_beyond_root(h)
+    own_heads(1)
+    for h in range(kv_heads // 2, kv_heads):
+        serve_anchor_beyond_root(h)
+    serve_ring(1, 0)
+    own_heads(2)
+    serve_ring(1, 1)
+    own_heads(3)
+    anchor_heads(0)
+    serve_ring(2, 0)
+    serve_y(1)
+    anchor_heads(1)
+    serve_ring(2, 1)
+    anchor_heads(2)
+    anchor_heads(3)
+    serve_ring(3, 0)
+    serve_y(2)
+    project(me)
+    own_sib.wait_recv()
+    project(me + 1 - 2 * core)
+    serve_ring(3, 1)
+    project_step(1)
+    serve_ring(4, 0)
+    serve_y(3)
+    project_step(2)
+    serve_ring(4, 1)
+    project_step(3)
+    serve_y(4)
+    project_step(4)
+    for copy in sent:
+        copy.wait_send()
+    for h in range(kv_heads):
+        for cond, copy in anchor_copies(h):
+            @pl.when(cond)
+            def _():
+                copy.wait_send()
+
+
+def fused(n, queries, keys, values, block_lengths, out_weight):
+    tokens, features = queries.shape
+    kv = keys.shape[1]
+    heads = features // HD
+    rows, width = out_weight.shape
+    half = n // 4
+    dma = pltpu.SemaphoreType.DMA
+    return pl.pallas_call(
+        functools.partial(kernel, n, "ctx"),
+        out_shape=jax.ShapeDtypeStruct((tokens, n * width), jnp.bfloat16),
+        in_specs=[pl.BlockSpec(memory_space=pltpu.SMEM)] + [pl.BlockSpec(memory_space=pl.ANY)] * 4,
+        out_specs=pl.BlockSpec(memory_space=pltpu.VMEM),
+        scratch_shapes=[
+            pltpu.VMEM((tokens, features), jnp.bfloat16),
+            pltpu.VMEM((tokens, kv), jnp.bfloat16),
+            pltpu.VMEM((tokens, kv), jnp.bfloat16),
+            pltpu.VMEM((tokens, kv), jnp.bfloat16),
+            pltpu.VMEM((tokens, kv), jnp.bfloat16),
+            pltpu.VMEM((n, rows, width), jnp.bfloat16),
+            pltpu.VMEM((tokens, features), jnp.float32),
+            pltpu.VMEM((heads, tokens, 1), jnp.float32),
+            pltpu.VMEM((heads, tokens, 1), jnp.float32),
+            pltpu.VMEM((tokens, features), jnp.bfloat16),
+            dma((2, half, 2)),
+            dma((2, half, 2)),
+            dma((2, half)),
+            dma((2, half)),
+            dma((2, half + 1, 3)),
+            dma((2, half + 1, 3)),
+            dma((kv // HD, 3, 2)),
+            dma((kv // HD, 2)),
+            dma((6,)),
+        ],
+        compiler_params=pltpu.CompilerParams(
+            collective_id=0, has_side_effects=True, vmem_limit_bytes=56 * 1024 * 1024
+        ),
+        name="attend_project",
+    )(block_lengths, queries, keys, values, out_weight)
 
 
 def broadcast(block, axis, source):
@@ -56,7 +376,7 @@
     return stacked.transpose(1, 0, 2, 3).reshape(row_count, key_heads * group_size * HD)
 
 
-def per_device(queries, keys, values, block_lengths, out_weight):
+def plain(queries, keys, values, block_lengths, out_weight):
     has_anchor = lax.axis_index("ctx") > 0
     anchor_keys, anchor_values = (broadcast(keys, "ctx", 0), broadcast(values, "ctx", 0))
     mixture = attend(
@@ -71,6 +391,13 @@
 
 
 def solution(mesh):
+    n = mesh.shape["ctx"]
+
+    def per_device(queries, keys, values, block_lengths, out_weight):
+        if n == 16 and mesh.shape["groups"] == 2 and out_weight.shape[1] % 128 == 0:
+            return fused(n, queries, keys, values, block_lengths, out_weight)
+        return plain(queries, keys, values, block_lengths, out_weight)
+
     return jax.shard_map(
         per_device,
         mesh=mesh,

time: 260 us -> 124 us (0.48); the launches traced: 257 us -> 124 us
  waiting for transfers between devices: 168 us -> 0 us
  Pallas kernels: 0 us -> 118 us
  matrix products: 64.7 us -> 0 us
  between operations: 14.1 us -> 0.66 us
  other arithmetic: 3.6 us -> 0 us
    pallas_call x0 -> x1, Pallas kernels: none -> 118 us  [fused(): pl.pallas_call(functools.partial(kernel, n, 'ctx'), out_shape=jax.ShapeDt...]
    psum x1 -> x0, waiting for transfers between devices: 87.3 us -> none  [broadcast(): return lax.psum(block, axis)]
    all_gather x1 -> x0, waiting for transfers between devices: 80.2 us -> none  [per_device(): lax.all_gather(out_weight, 'ctx', axis=1, tiled=True)]
    dot_general x5 -> x0, matrix products: 34.8 us -> none  [the longest x4 20.4 us: one_head(): jnp.einsum('gqk,kd->qgd', soft_weights, head_values, preferred_element_ty...]
    sub x4 -> x0, matrix products: 29.9 us -> none  [one_head(): exponent = jnp.exp(scores - row_top)]
  transfers between devices with their start and end apart: 2 -> 0, of which waited for: 2 -> 0; matrix products, arithmetic and copies ran while one was open for 22% -> 0% of each run, Pallas kernels for 0% -> 0%
where the time goes in v1:
time: 124 us
  Pallas kernels  118 us (95%)
  local copies, waits for them, and re-layouts  4.7 us (4%)
    pallas_call x1, Pallas kernels, fused(): pl.pallas_call(functools.partial(kernel, n, 'ctx'), out_shape=jax.ShapeDt...  118 us
    unnamed x1, local copies, waits for them, and re-layouts  4.7 us

profile of v1, /device:TPU:25, one launch (start us, length us, event | category | flops | bytes accessed | tf_op | source)
XLA Modules:
  0.0 123.5 jit_solution(1560597782322686641)
XLA Ops:
  0.7 118.1 %attend_project.1 = bf16[512,4096]{1,0:T(8,128)(2,1)} custom-call(s32[1]{0:T(128)S(6)} %copy.7.length_ref, bf16[512,2048]{1,0:T(8,128)(2,1)} %q_hbm.1, bf16[512,512]{1,0:T(8,128)(2,1)} %k_hbm.1, bf16[512,512]{1,0:T(8,128)(2,1)} %v_hbm.1, bf16[2048,256]{1,0:T(8,128)(2,1)} %w_hbm.1), custom_call_target="tpu_custom_call" | custom-call | tf_op jit(solution)/shard_map/attend_project/pallas_call | solution.py:298
  118.8 4.7 %copy.8 = bf16[512,4096]{1,0:T(8,128)(2,1)} copy(bf16[512,4096]{1,0:T(8,128)(2,1)} %attend_project.1) | data formatting | bytes 8388608

commit v2 on v1

--- a/solution.py
+++ b/solution.py
@@ -103,27 +103,21 @@
                 start(sib_copy(d, s, 2))
 
     root = me == 0
+    chunks = 4
+    chunk = tokens // chunks
 
     def anchor_copies(h):
-        k = h * 2 // kv_heads
-        cols = pl.ds(h * HD, HD)
+        k = h * 2 // chunks
+        part = pl.ds(h * chunk, chunk)
         lead = (core == 0) & (x == k)
         z_cond = lead & (z < half - 1)
         x_cond = lead if k == 0 else (lead & (z > 0)) | root
         found = []
         for kind, (cond, device) in enumerate(((z_cond, above), (x_cond, cross), (core == 0, sibling))):
             for t, ref in enumerate((ak_ref, av_ref)):
-                view = ref.at[:, cols]
+                view = ref.at[part, :]
                 found.append((cond, remote(view, view, anchor_send.at[h, kind, t], anchor_recv.at[h, t], device)))
         return found
-
-    def serve_anchor(h):
-        @pl.when(me > 0)
-        def _():
-            for t, ref in enumerate((ak_ref, av_ref)):
-                view = ref.at[:, pl.ds(h * HD, HD)]
-                remote(view, view, anchor_send.at[h, 0, t], anchor_recv.at[h, t], sibling).wait_recv()
-        send_anchor(h)
 
     def send_anchor(h):
         for cond, copy in anchor_copies(h):
@@ -158,22 +152,25 @@
     def _():
         for load in root_loads:
             load.wait()
-        for h in range(kv_heads):
+        for h in (0, 2, 1, 3):
             send_anchor(h)
 
-    for piece in (0, 1):
-        for d in (RIGHT, LEFT):
-            if has(d, 1, piece):
-                start(ring_copy(d, 1, piece))
-    start(own_sib)
+    firsts = [ring_copy(d, 1, piece) for piece in (0, 1) for d in (RIGHT, LEFT)] + [own_sib]
+    sent.extend(firsts)
+
+    @pl.when(core == 1)
+    def _():
+        for copy in firsts:
+            copy.start()
+
     for load in loads:
         load.wait()
 
-    def serve_anchor_beyond_root(h):
+    def serve_anchor(h):
         @pl.when(me > 0)
         def _():
             for t, ref in enumerate((ak_ref, av_ref)):
-                view = ref.at[:, pl.ds(h * HD, HD)]
+                view = ref.at[pl.ds(h * chunk, chunk), :]
                 remote(view, view, anchor_send.at[h, 0, t], anchor_recv.at[h, t], sibling).wait_recv()
             send_anchor(h)
 
@@ -249,39 +246,59 @@
             project(chip_at(pos - turn * s) * 2 + (i + core) % 2)
 
     own_heads(0)
-    for h in range(kv_heads // 2):
-        serve_anchor_beyond_root(h)
+
+    @pl.when(core == 0)
+    def _():
+        for k in (0, 1):
+            @pl.when(x == k)
+            def _():
+                serve_anchor(2 * k)
+                serve_anchor(2 * k + 1)
+        for copy in firsts:
+            copy.start()
     own_heads(1)
-    for h in range(kv_heads // 2, kv_heads):
-        serve_anchor_beyond_root(h)
-    serve_ring(1, 0)
+    serve_ring(1,0)
+
+    @pl.when(core == 0)
+    def _():
+        for k in (0, 1):
+            @pl.when(x != k)
+            def _():
+                serve_anchor(2 * k)
+                serve_anchor(2 * k + 1)
     own_heads(2)
-    serve_ring(1, 1)
+    serve_ring(1,1)
     own_heads(3)
+    serve_ring(2,0)
+    serve_y(1)
+
+    @pl.when(core == 1)
+    def _():
+        for h in range(chunks):
+            serve_anchor(h)
+
     anchor_heads(0)
-    serve_ring(2, 0)
-    serve_y(1)
     anchor_heads(1)
-    serve_ring(2, 1)
+    serve_ring(2,1)
     anchor_heads(2)
+    serve_ring(3,0)
+    serve_y(2)
     anchor_heads(3)
-    serve_ring(3, 0)
-    serve_y(2)
+    serve_ring(3,1)
     project(me)
     own_sib.wait_recv()
     project(me + 1 - 2 * core)
-    serve_ring(3, 1)
     project_step(1)
-    serve_ring(4, 0)
+    serve_ring(4,0)
     serve_y(3)
     project_step(2)
-    serve_ring(4, 1)
+    serve_ring(4,1)
     project_step(3)
     serve_y(4)
     project_step(4)
     for copy in sent:
         copy.wait_send()
-    for h in range(kv_heads):
+    for h in range(chunks):
         for cond, copy in anchor_copies(h):
             @pl.when(cond)
             def _():
@@ -317,8 +334,8 @@
             dma((2, half)),
             dma((2, half + 1, 3)),
             dma((2, half + 1, 3)),
-            dma((kv // HD, 3, 2)),
-            dma((kv // HD, 2)),
+            dma((4, 3, 2)),
+            dma((4, 2)),
             dma((6,)),
         ],
         compiler_params=pltpu.CompilerParams(

time: 124 us -> 106 us (0.85)
  Pallas kernels: 118 us -> 100 us
    pallas_call x1, Pallas kernels: 118 us -> 100 us  [fused(): pl.pallas_call(functools.partial(kernel, n, 'ctx'), out_shape=jax.ShapeDt...]
where the time goes in v2:
time: 106 us
  Pallas kernels  100 us (94%)
  local copies, waits for them, and re-layouts  4.7 us (4%)
    pallas_call x1, Pallas kernels, fused(): pl.pallas_call(functools.partial(kernel, n, 'ctx'), out_shape=jax.ShapeDt...  100 us
    unnamed x1, local copies, waits for them, and re-layouts  4.7 us

profile of v2, /device:TPU:25, one launch (start us, length us, event | category | flops | bytes accessed | tf_op | source)
XLA Modules:
  0.0 105.7 jit_solution(7499657427568785859)
XLA Ops:
  0.7 100.3 %attend_project.1 = bf16[512,4096]{1,0:T(8,128)(2,1)} custom-call(s32[1]{0:T(128)S(6)} %copy.7.length_ref, bf16[512,2048]{1,0:T(8,128)(2,1)} %q_hbm.1, bf16[512,512]{1,0:T(8,128)(2,1)} %k_hbm.1, bf16[512,512]{1,0:T(8,128)(2,1)} %v_hbm.1, bf16[2048,256]{1,0:T(8,128)(2,1)} %w_hbm.1), custom_call_target="tpu_custom_call" | custom-call | tf_op jit(solution)/shard_map/attend_project/pallas_call | solution.py:315
  101.0 4.7 %copy.8 = bf16[512,4096]{1,0:T(8,128)(2,1)} copy(bf16[512,4096]{1,0:T(8,128)(2,1)} %attend_project.1) | data formatting | bytes 8388608
